TPU v7x, 32 devices: a whole 2x2x4 slice. The times are simulated.
32 devices in a mesh: ha: 8 (over z, core), wa: 4 (over y, x).
Axes of the slice: x: 2, y: 2, z: 4, core: 2. Of those that a mesh axis runs over, the one named last changes fastest.
Arguments:
- latents: bfloat16 [64, 64, 64, 512], P('ha', 'wa'), may hold values from -8 to 8
- cotangent: bfloat16 [64, 64, 64, 512], P('ha', 'wa'), may hold values from -0.59765625 to 0.59765625
- w_down: bfloat16 [512, 18], replicated, may hold values from -0.25 to 0.25
- bit_bias: float32 [18], replicated, may hold values from -1.5 to 1.5
- w_up: bfloat16 [18, 512], replicated, may hold values from -1.5 to 1.5
Outputs:
- grad_latents: bfloat16 [64, 64, 64, 512], P('ha', 'wa')
- bit_entropy: float32 [64, 64, 64], P('ha', 'wa')
- marginal: float32 [18], replicated
- grad_down: float32 [512, 18], replicated
- grad_bias: float32 [18], replicated
- grad_up: float32 [18, 512], replicated
All inputs are finite; a program needn't handle non-finite values.
Results may differ from a plain program's by a relative error of at most 0.005.
Values may be sent and summed in bfloat16 or wider, within the bound.
No kernel may reach another device: no remote copies, remote signals or barrier semaphores. Data moves between devices by JAX's collectives and lax.ppermute only.
A program may use at most 128 MiB of HBM per device.

v0:
```python
import jax
import jax.numpy as jnp
from jax import lax
from jax.sharding import PartitionSpec as P

local_weight = 4.0
margin_weight = 4.0


def extended_2(cells, sides, width):
    for axis, dim in sides:
        count = lax.axis_size(axis)
        head = lax.slice_in_dim(cells, 0, width, axis=dim)
        tail = lax.slice_in_dim(cells, cells.shape[dim] - width, cells.shape[dim], axis=dim)
        cells = jnp.concatenate(
            [
                lax.ppermute(tail, axis, [(i, (i + 1) % count) for i in range(count)]),
                cells,
                lax.ppermute(head, axis, [((i + 1) % count, i) for i in range(count)]),
            ],
            axis=dim,
        )
    return cells


def window(extended, rows, cols):
    total = extended[0:rows, 0:cols]
    for first in range(3):
        for second in range(3):
            if first or second:
                total = total + extended[first : first + rows, second : second + cols]
    return total / 9.0


def binary(values):
    return -values * jnp.log(values) - (1.0 - values) * jnp.log1p(-values)


def local(latents, cotangent, w_down, bit_bias, w_up):
    rows, cols, images, width = latents.shape
    bits = w_down.shape[1]
    count = rows * cols * images * lax.axis_size("ha") * lax.axis_size("wa")
    flattened = latents.reshape(-1, width)
    outward = cotangent.reshape(-1, width)
    layers = 1
    logits = jnp.dot(flattened, w_down, preferred_element_type=jnp.float32) + bit_bias
    squash = jax.nn.sigmoid(logits)
    prob = 0.01 + 0.98 * squash
    wide_prob = extended_2(prob.reshape(rows, cols, images, bits), (("ha", 0), ("wa", 1)), layers)
    local_mass = jnp.sum(prob, axis=0) / count
    marginal = lax.psum(local_mass, ("ha", "wa"))
    wide_pooled = window(wide_prob, rows + 2 * layers - 2, cols + 2 * layers - 2)
    slope = local_weight * jnp.log((1.0 - wide_pooled) / wide_pooled)
    wide_slope = extended_2(slope, (("ha", 0), ("wa", 1)), 1)
    bit_entropy = jnp.sum(binary(wide_pooled), axis=-1)
    code = (2.0 * squash - 1.0).astype(jnp.bfloat16)
    code_grad = jnp.dot(outward, w_up.T, preferred_element_type=jnp.float32)
    spread = window(wide_slope, rows, cols).reshape(-1, bits)
    steepness = squash * (1.0 - squash)
    base = ((2.0 * code_grad + 0.98 * spread) * steepness).astype(jnp.bfloat16)
    stacked = jnp.concatenate([base, steepness.astype(jnp.bfloat16)], axis=1)
    latent_part = (
        lax.dot_general(
            flattened, stacked, (((0,), (0,)), ((), ())), preferred_element_type=jnp.float32
        )
        / count
    )
    column_part = jnp.sum(stacked.astype(jnp.float32), axis=0) / count
    up_part = (
        lax.dot_general(code, outward, (((0,), (0,)), ((), ())), preferred_element_type=jnp.float32)
        / count
    )
    latent_total, column_total, grad_up = lax.psum(
        (latent_part, column_part, up_part), ("ha", "wa")
    )
    drift = margin_weight * jnp.log((1.0 - marginal) / marginal)
    logit_grad = ((2.0 * code_grad + 0.98 * (spread - drift)) * steepness).astype(jnp.bfloat16)
    grad_latents = jnp.dot(logit_grad, w_down.T, preferred_element_type=jnp.float32).astype(
        jnp.bfloat16
    )
    grad_latents = grad_latents.reshape(latents.shape)
    grad_down = latent_total[:, :bits] - 0.98 * drift * latent_total[:, bits:]
    grad_bias = column_total[:bits] - 0.98 * drift * column_total[bits:]
    return (grad_latents, bit_entropy, marginal, grad_down, grad_bias, grad_up)


def solution(mesh):
    placed = (P("ha", "wa", None, None), P("ha", "wa", None, None), P(), P(), P())
    return jax.shard_map(
        local,
        mesh=mesh,
        in_specs=placed,
        out_specs=(P("ha", "wa", None, None), P("ha", "wa", None), P(), P(), P(), P()),
        check_vma=False,
    )
```

profile of v0, /device:TPU:8, one launch (start us, length us, event | category | flops | bytes accessed | tf_op | source)
XLA Modules:
  0.0 191.5 jit_solution(5777653072572231376)
XLA Ops:
  7.2 0.0 copy-start
  7.2 0.0 all-reduce.3.cloned.1.call-start
  7.2 0.7 copy-done
  7.9 5.7 %multiply_add_fusion = (f32[8192,18]{0,1:T(8,128)S(1)}, f32[8192,18]{0,1:T(8,128)S(1)}) fusion(f32[18]{0:T(128)} %param.8, bf16[8192,512]{1,0:T(8,128)(2,1)} %bitcast.26, bf16[512,18]{0,1:T(8,128)(2,1)S(1)} %copy-done), kind=kOutput, calls=%fused_computation.59 | convolution fusion | flops 151879680 | bytes 9586760 | tf_op jit(solution)/shard_map/dot_general | solution.py:46
  13.6 0.1 slice.107
  13.7 0.0 collective-permute-start
  13.8 0.1 slice.109
  13.9 1.8 collective-permute-start.1
  15.6 0.5 reshape.34
  16.1 2.2 %collective-permute-done = f32[1,16,64,18]{2,1,0,3:T(8,128)S(1)} collective-permute-done((f32[1,16,64,18]{2,1,0,3:T(8,128)S(1)}, f32[1,16,64,18]{2,1,0,3:T(8,128)S(1)}, u32[]{:S(2)}, u32[]{:S(2)}) %collective-permute-start) | collective-permute-done | bytes 73760 | tf_op jit(solution)/shard_map/ppermute | solution.py:17
  18.3 0.1 constant_dynamic-update-slice_fusion.1
  18.4 0.7 collective-permute-done.1
  19.2 0.1 fusion.42
  19.3 2.0 %collective-permute-start.2 = (f32[10,1,64,18]{2,1,0,3:T(1,128)S(1)}, f32[10,1,64,18]{2,1,0,3:T(1,128)S(1)}, u32[]{:S(2)}, u32[]{:S(2)}) collective-permute-start(f32[10,1,64,18]{2,1,0,3:T(1,128)S(1)} %get-tuple-element.17), channel_id=1, source_target_pairs={{0,1},{1,2},{2,3},{3,0},{4,5},{5,6},{6,7},{7,4},{8,9},{9,10},{10,1... | collective-permute-start | bytes 138248 | tf_op jit(solution)/shard_map/ppermute | solution.py:17
  21.4 1.0 collective-permute-start.3
  22.4 3.3 %collective-permute-done.2 = f32[10,1,64,18]{2,1,0,3:T(1,128)S(1)} collective-permute-done((f32[10,1,64,18]{2,1,0,3:T(1,128)S(1)}, f32[10,1,64,18]{2,1,0,3:T(1,128)S(1)}, u32[]{:S(2)}, u32[]{:S(2)}) %collective-permute-start.2) | collective-permute-done | bytes 46112 | tf_op jit(solution)/shard_map/ppermute | solution.py:17
  25.7 2.5 %collective-permute-done.3 = f32[10,1,64,18]{2,1,0,3:T(1,128)S(1)} collective-permute-done((f32[10,1,64,18]{2,1,0,3:T(1,128)S(1)}, f32[10,1,64,18]{2,1,0,3:T(1,128)S(1)}, u32[]{:S(2)}, u32[]{:S(2)}) %collective-permute-start.3) | collective-permute-done | bytes 46112 | tf_op jit(solution)/shard_map/ppermute | solution.py:19
  28.2 3.1 %fusion.7 = (f32[8,16,64]{2,1,0:T(8,128)}, f32[8,16,64,18]{2,1,0,3:T(8,128)S(1)}) fusion(f32[10,1,64,18]{2,1,0,3:T(1,128)S(1)} %collective-permute-done.3, f32[10,16,64,18]{2,1,0,3:T(8,128)S(1)} %constant_dynamic-update-slice_fusion, f32[1,16,64,18]{2,1,0,3:T(8,128)S(1)} %collective-permute-done.1, f32[8,16,64,18]{2,1,0,3:T(8,128)S(1)} %reshape.34, ...), kind=kLoop, calls=%fused_computation.24 | loop fusion | flops 3383296 | bytes 2189312 | tf_op jit(solution)/shard_map/reduce_sum | solution.py:55
  31.4 0.3 fusion.5
  31.7 0.1 collective-permute-start.4
  31.8 1.7 collective-permute-start.5
  33.5 2.8 %collective-permute-done.4 = f32[1,16,64,18]{2,1,0,3:T(8,128)S(1)} collective-permute-done((f32[1,16,64,18]{2,1,0,3:T(8,128)S(1)}, f32[1,16,64,18]{2,1,0,3:T(8,128)S(1)}, u32[]{:S(2)}, u32[]{:S(2)}) %collective-permute-start.4) | collective-permute-done | bytes 73760 | tf_op jit(solution)/shard_map/ppermute | solution.py:17
  36.3 0.7 collective-permute-done.5
  37.0 0.2 pad_maximum_fusion.11
  37.2 1.6 collective-permute-start.6
  38.8 1.4 collective-permute-start.7
  40.2 4.6 %convolution_multiply_fusion.2 = f32[18,512]{1,0:T(8,128)S(1)} fusion(bf16[8192,512]{1,0:T(8,128)(2,1)} %bitcast.24, f32[8192,18]{0,1:T(8,128)S(1)} %get-tuple-element.29), kind=kOutput, calls=%fused_computation.55 | convolution fusion | flops 151446528 | bytes 9015296 | tf_op jit(solution)/shard_map/dot_general | solution.py:70
  44.7 0.0 collective-permute-done.6
  44.8 0.0 collective-permute-done.7
  44.8 0.4 maximum_maximum_fusion
  45.2 0.7 fusion.21
  45.9 0.0 copy-start.1
  45.9 0.4 reshape.35
  46.3 0.3 copy-done.1
  46.7 5.8 %multiply_convert_fusion = (bf16[8192,18]{0,1:T(8,128)(2,1)S(1)}, f32[18]{0:T(128)S(1)}, bf16[8192,18]{0,1:T(8,128)(2,1)S(1)}, f32[8192,18]{0,1:T(8,128)S(1)}) fusion(f32[8192,18]{0,1:T(8,128)S(1)} %reshape.35, f32[8192,18]{0,1:T(8,128)S(1)} %get-tuple-element.29, bf16[8192,512]{1,0:T(8,128)(2,1)} %bitcast.25, bf16[18,512]{1,0:T(8,128)(2,1)S(1)} %copy-done.1), kind=kOutput, calls=%fused_computation.57 | convolution fusion | flops 152616944 | bytes 10766408 | tf_op jit(solution)/shard_map/dot_general | solution.py:57
  52.5 0.3 convert_reduce_fusion
  52.7 5.3 %fusion.25 = f32[512,36]{0,1:T(8,128)} fusion(bf16[8192,512]{1,0:T(8,128)(2,1)} %bitcast.27, bf16[8192,18]{0,1:T(8,128)(2,1)S(1)} %get-tuple-element.23, bf16[8192,18]{0,1:T(8,128)(2,1)S(1)} %get-tuple-element.21), kind=kOutput, calls=%fused_computation.54 | convolution fusion | flops 303187968 | bytes 9052160 | tf_op jit(solution)/shard_map/dot_general | solution.py:63
  58.0 0.0 all-reduce.3.cloned.1.call-update
  58.1 42.2 %all-reduce = (f32[18]{0:T(128)S(1)}, f32[36]{0:T(128)S(1)}, f32[18,512]{1,0:T(8,128)}) all-reduce(f32[18]{0:T(128)S(1)} %broadcast_multiply_fusion.3, f32[36]{0:T(128)S(1)} %broadcast_multiply_fusion, f32[18,512]{1,0:T(8,128)S(1)} %convolution_multiply_fusion.2), channel_id=1, replica_groups=mesh['ha'=8,'wa'=4] {'ha','wa'}, use_global_device_ids=true, to_apply=%region_1.0 | all-reduce | flops 9270 | bytes 74160 | tf_op jit(solution)/shard_map/psum | solution.py:51
  100.2 0.0 copy-start.2
  100.2 0.6 multiply_subtract_fusion
  100.8 5.9 %convolution_convert_fusion = bf16[8192,512]{1,0:T(8,128)(2,1)} fusion(bf16[512,18]{0,1:T(8,128)(2,1)S(1)} %copy-done, f32[8192,18]{0,1:T(8,128)S(1)} %get-tuple-element.30, f32[8192,18]{0,1:T(8,128)S(1)} %reshape.35, f32[8192,18]{0,1:T(8,128)S(1)} %get-tuple-element.29, f32[18]{0:T(128)S(1)} %get-tuple-element.27), kind=kOutput, calls=%fused_computation | convolution fusion | flops 156221440 | bytes 10176584 | tf_op jit(solution)/shard_map/dot_general | solution.py:78
  106.7 0.0 copy-done.2
  106.7 76.4 %all-reduce.3.cloned.1.call-done = f32[512,36]{0,1:T(8,128)} async-done(((f32[512,36]{0,1:T(8,128)}), f32[512,36]{0,1:T(8,128)}) %all-reduce.3.cloned.1.call-update) | async-done | bytes 73744 | tf_op jit(solution)/shard_map/psum | solution.py:73
  183.1 1.6 fusion.32
  (7 shorter events, 0.1 us)
Async XLA Ops:
  7.2 0.7 copy-start
  7.2 176.0 %all-reduce.3.cloned.1.call-start = ((), (), s32[]{:S(2)}) async-start(), calls=%async_computation | async-start | bytes 163840 | tf_op jit(solution)/shard_map/psum | solution.py:73
  13.7 4.6 %collective-permute-start = (f32[1,16,64,18]{2,1,0,3:T(8,128)S(1)}, f32[1,16,64,18]{2,1,0,3:T(8,128)S(1)}, u32[]{:S(2)}, u32[]{:S(2)}) collective-permute-start(f32[1,16,64,18]{2,1,0,3:T(8,128)S(1)} %bitcast.29), channel_id=1, source_target_pairs={{0,4},{4,8},{8,12},{12,16},{16,20},{20,24},{24,28},{28,0},{1,5},{5... | collective-permute-start | bytes 221192 | tf_op jit(solution)/shard_map/ppermute | solution.py:17
  13.9 5.3 %collective-permute-start.1 = (f32[1,16,64,18]{2,1,0,3:T(8,128)S(1)}, f32[1,16,64,18]{2,1,0,3:T(8,128)S(1)}, u32[]{:S(2)}, u32[]{:S(2)}) collective-permute-start(f32[1,16,64,18]{2,1,0,3:T(8,128)S(1)} %bitcast.30), channel_id=1, source_target_pairs={{4,0},{8,4},{12,8},{16,12},{20,16},{24,20},{28,24},{0,28},{5,1},{9... | collective-permute-start | bytes 221192 | tf_op jit(solution)/shard_map/ppermute | solution.py:19
  19.3 6.4 %collective-permute-start.2 = (f32[10,1,64,18]{2,1,0,3:T(1,128)S(1)}, f32[10,1,64,18]{2,1,0,3:T(1,128)S(1)}, u32[]{:S(2)}, u32[]{:S(2)}) collective-permute-start(f32[10,1,64,18]{2,1,0,3:T(1,128)S(1)} %get-tuple-element.17), channel_id=1, source_target_pairs={{0,1},{1,2},{2,3},{3,0},{4,5},{5,6},{6,7},{7,4},{8,9},{9,10},{10,1... | collective-permute-start | bytes 138248 | tf_op jit(solution)/shard_map/ppermute | solution.py:17
  21.4 6.8 %collective-permute-start.3 = (f32[10,1,64,18]{2,1,0,3:T(1,128)S(1)}, f32[10,1,64,18]{2,1,0,3:T(1,128)S(1)}, u32[]{:S(2)}, u32[]{:S(2)}) collective-permute-start(f32[10,1,64,18]{2,1,0,3:T(1,128)S(1)} %get-tuple-element.18), channel_id=1, source_target_pairs={{1,0},{2,1},{3,2},{0,3},{5,4},{6,5},{7,6},{4,7},{9,8},{10,9},{11,1... | collective-permute-start | bytes 138248 | tf_op jit(solution)/shard_map/ppermute | solution.py:19
  31.7 4.6 %collective-permute-start.4 = (f32[1,16,64,18]{2,1,0,3:T(8,128)S(1)}, f32[1,16,64,18]{2,1,0,3:T(8,128)S(1)}, u32[]{:S(2)}, u32[]{:S(2)}) collective-permute-start(f32[1,16,64,18]{2,1,0,3:T(8,128)S(1)} %get-tuple-element.19), channel_id=1, source_target_pairs={{0,4},{4,8},{8,12},{12,16},{16,20},{20,24},{24,28},{28,0},{1,5},{5... | collective-permute-start | bytes 221192 | tf_op jit(solution)/shard_map/ppermute | solution.py:17
  31.8 5.3 %collective-permute-start.5 = (f32[1,16,64,18]{2,1,0,3:T(8,128)S(1)}, f32[1,16,64,18]{2,1,0,3:T(8,128)S(1)}, u32[]{:S(2)}, u32[]{:S(2)}) collective-permute-start(f32[1,16,64,18]{2,1,0,3:T(8,128)S(1)} %get-tuple-element.20), channel_id=1, source_target_pairs={{4,0},{8,4},{12,8},{16,12},{20,16},{24,20},{28,24},{0,28},{5,1},{9... | collective-permute-start | bytes 221192 | tf_op jit(solution)/shard_map/ppermute | solution.py:19
  37.2 7.6 %collective-permute-start.6 = (f32[10,1,64,18]{2,1,0,3:T(1,128)S(1)}, f32[10,1,64,18]{2,1,0,3:T(1,128)S(1)}, u32[]{:S(2)}, u32[]{:S(2)}) collective-permute-start(f32[10,1,64,18]{2,1,0,3:T(1,128)S(1)} %get-tuple-element.15), channel_id=1, source_target_pairs={{0,1},{1,2},{2,3},{3,0},{4,5},{5,6},{6,7},{7,4},{8,9},{9,10},{10,1... | collective-permute-start | bytes 138248 | tf_op jit(solution)/shard_map/ppermute | solution.py:17
  38.8 6.0 %collective-permute-start.7 = (f32[10,1,64,18]{2,1,0,3:T(1,128)S(1)}, f32[10,1,64,18]{2,1,0,3:T(1,128)S(1)}, u32[]{:S(2)}, u32[]{:S(2)}) collective-permute-start(f32[10,1,64,18]{2,1,0,3:T(1,128)S(1)} %get-tuple-element.16), channel_id=1, source_target_pairs={{1,0},{2,1},{3,2},{0,3},{5,4},{6,5},{7,6},{4,7},{9,8},{10,9},{11,1... | collective-permute-start | bytes 138248 | tf_op jit(solution)/shard_map/ppermute | solution.py:19
  45.9 0.7 copy-start.1
  100.2 6.5 %copy-start.2 = (f32[18]{0:T(128)}, f32[18]{0:T(128)S(1)}, u32[]{:S(2)}) copy-start(f32[18]{0:T(128)S(1)} %get-tuple-element.6) | copy-start | bytes 220
Sparse Core Ops, SparseCore 0:
  58.2 124.8 all-reduce.2
where the time goes:
time: 192 us
  waiting for transfers between devices  88.8 us (46%)
  blocking collectives  42.2 us (22%)
  matrix products  27.2 us (14%)
  between operations  14.2 us (7%)
  starting transfers between devices  9.68 us (5%)
  other arithmetic  7.18 us (4%)
  local copies, waits for them, and re-layouts  2.33 us (1%)
    psum x1, waiting for transfers between devices, local(): lax.psum((latent_part, column_part, up_part), ('ha', 'wa'))  76.4 us
    psum x1, blocking collectives, local(): marginal = lax.psum(local_mass, ('ha', 'wa'))  42.2 us
    ppermute x4, waiting for transfers between devices, extended_2(): lax.ppermute(tail, axis, [(i, (i + 1) % count) for i in range(count)])  8.36 us
    ppermute x4, starting transfers between devices, extended_2(): lax.ppermute(head, axis, [((i + 1) % count, i) for i in range(count)])  5.91 us
    dot_general x1, matrix products, local(): jnp.dot(logit_grad, w_down.T, preferred_element_type=jnp.float32)  5.89 us
    dot_general x1, matrix products, local(): code_grad = jnp.dot(outward, w_up.T, preferred_element_type=jnp.float32)  5.8 us
    dot_general x1, matrix products, local(): jnp.dot(flattened, w_down, preferred_element_type=jnp.float32) + bit_bias  5.7 us
    dot_general x1, matrix products, local(): lax.dot_general(flattened, stacked, (((0,), (0,)), ((), ())), preferred_e...  5.3 us
  transfers between devices with their start and end apart: 9, of which 7 were waited for; matrix products, arithmetic and copies ran while one was open for 6% of the time, Pallas kernels for 0%

commit v1 on v0

--- a/solution.py
+++ b/solution.py
@@ -48,7 +48,7 @@
     prob = 0.01 + 0.98 * squash
     wide_prob = extended_2(prob.reshape(rows, cols, images, bits), (("ha", 0), ("wa", 1)), layers)
     local_mass = jnp.sum(prob, axis=0) / count
-    marginal = lax.psum(local_mass, ("ha", "wa"))
+    marginal = lax.psum(lax.psum(local_mass, "ha"), "wa")
     wide_pooled = window(wide_prob, rows + 2 * layers - 2, cols + 2 * layers - 2)
     slope = local_weight * jnp.log((1.0 - wide_pooled) / wide_pooled)
     wide_slope = extended_2(slope, (("ha", 0), ("wa", 1)), 1)

time: 192 us -> 206 us (1.073)
  blocking collectives: 42.2 us -> 65.6 us
  waiting for transfers between devices: 88.8 us -> 79.4 us
    psum x1 -> x3, blocking collectives: 42.2 us -> 65.6 us  [the longest x1 42.9 us: local(): lax.psum((latent_part, column_part, up_part), ('ha', 'wa'))]
    psum x1, waiting for transfers between devices: 76.4 us -> 67.1 us  [local(): lax.psum((latent_part, column_part, up_part), ('ha', 'wa'))]
where the time goes in v1:
time: 206 us
  waiting for transfers between devices  79.4 us (39%)
  blocking collectives  65.6 us (32%)
  matrix products  27.3 us (13%)
  between operations  14.2 us (7%)
  starting transfers between devices  9.68 us (5%)
  other arithmetic  7.18 us (3%)
  local copies, waits for them, and re-layouts  2.33 us (1%)
    psum x1, waiting for transfers between devices, local(): lax.psum((latent_part, column_part, up_part), ('ha', 'wa'))  67.1 us
    psum x1, blocking collectives, local(): lax.psum((latent_part, column_part, up_part), ('ha', 'wa'))  42.9 us
    psum x2, blocking collectives, local(): marginal = lax.psum(lax.psum(local_mass, 'ha'), 'wa')  22.7 us
    ppermute x4, waiting for transfers between devices, extended_2(): lax.ppermute(tail, axis, [(i, (i + 1) % count) for i in range(count)])  8.36 us
    ppermute x4, starting transfers between devices, extended_2(): lax.ppermute(head, axis, [((i + 1) % count, i) for i in range(count)])  5.91 us
    dot_general x1, matrix products, local(): jnp.dot(logit_grad, w_down.T, preferred_element_type=jnp.float32)  5.89 us
    dot_general x1, matrix products, local(): code_grad = jnp.dot(outward, w_up.T, preferred_element_type=jnp.float32)  5.8 us
    dot_general x1, matrix products, local(): jnp.dot(flattened, w_down, preferred_element_type=jnp.float32) + bit_bias  5.7 us
  transfers between devices with their start and end apart: 9, of which 7 were waited for; matrix products, arithmetic and copies ran while one was open for 6% of the time, Pallas kernels for 0%

profile of v1, /device:TPU:8, one launch (start us, length us, event | category | flops | bytes accessed | tf_op | source)
XLA Modules:
  0.0 205.7 jit_solution(18036042748925786709)
XLA Ops:
  7.2 0.0 copy-start
  7.2 0.0 all-reduce.3.cloned.1.call-start
  7.2 0.7 copy-done
  7.9 5.7 %multiply_add_fusion = (f32[8192,18]{0,1:T(8,128)S(1)}, f32[8192,18]{0,1:T(8,128)S(1)}) fusion(f32[18]{0:T(128)} %param.8, bf16[8192,512]{1,0:T(8,128)(2,1)} %bitcast.26, bf16[512,18]{0,1:T(8,128)(2,1)S(1)} %copy-done), kind=kOutput, calls=%fused_computation.59 | convolution fusion | flops 151879680 | bytes 9586760 | tf_op jit(solution)/shard_map/dot_general | solution.py:46
  13.6 0.1 slice.107
  13.7 0.0 collective-permute-start
  13.8 0.1 slice.109
  13.9 1.8 collective-permute-start.1
  15.6 0.5 reshape.34
  16.1 2.2 %collective-permute-done = f32[1,16,64,18]{2,1,0,3:T(8,128)S(1)} collective-permute-done((f32[1,16,64,18]{2,1,0,3:T(8,128)S(1)}, f32[1,16,64,18]{2,1,0,3:T(8,128)S(1)}, u32[]{:S(2)}, u32[]{:S(2)}) %collective-permute-start) | collective-permute-done | bytes 73760 | tf_op jit(solution)/shard_map/ppermute | solution.py:17
  18.3 0.1 constant_dynamic-update-slice_fusion.1
  18.4 0.7 collective-permute-done.1
  19.2 0.1 fusion.42
  19.3 2.0 collective-permute-start.2
  21.4 1.0 collective-permute-start.3
  22.4 3.3 %collective-permute-done.2 = f32[10,1,64,18]{2,1,0,3:T(1,128)S(1)} collective-permute-done((f32[10,1,64,18]{2,1,0,3:T(1,128)S(1)}, f32[10,1,64,18]{2,1,0,3:T(1,128)S(1)}, u32[]{:S(2)}, u32[]{:S(2)}) %collective-permute-start.2) | collective-permute-done | bytes 46112 | tf_op jit(solution)/shard_map/ppermute | solution.py:17
  25.7 2.5 %collective-permute-done.3 = f32[10,1,64,18]{2,1,0,3:T(1,128)S(1)} collective-permute-done((f32[10,1,64,18]{2,1,0,3:T(1,128)S(1)}, f32[10,1,64,18]{2,1,0,3:T(1,128)S(1)}, u32[]{:S(2)}, u32[]{:S(2)}) %collective-permute-start.3) | collective-permute-done | bytes 46112 | tf_op jit(solution)/shard_map/ppermute | solution.py:19
  28.2 3.1 %fusion.7 = (f32[8,16,64]{2,1,0:T(8,128)}, f32[8,16,64,18]{2,1,0,3:T(8,128)S(1)}) fusion(f32[10,1,64,18]{2,1,0,3:T(1,128)S(1)} %collective-permute-done.3, f32[10,16,64,18]{2,1,0,3:T(8,128)S(1)} %constant_dynamic-update-slice_fusion, f32[1,16,64,18]{2,1,0,3:T(8,128)S(1)} %collective-permute-done.1, f32[8,16,64,18]{2,1,0,3:T(8,128)S(1)} %reshape.34, ...), kind=kLoop, calls=%fused_computation.24 | loop fusion | flops 3383296 | bytes 2189312 | tf_op jit(solution)/shard_map/reduce_sum | solution.py:55
  31.4 0.3 fusion.5
  31.7 0.1 collective-permute-start.4
  31.8 1.7 collective-permute-start.5
  33.5 2.8 %collective-permute-done.4 = f32[1,16,64,18]{2,1,0,3:T(8,128)S(1)} collective-permute-done((f32[1,16,64,18]{2,1,0,3:T(8,128)S(1)}, f32[1,16,64,18]{2,1,0,3:T(8,128)S(1)}, u32[]{:S(2)}, u32[]{:S(2)}) %collective-permute-start.4) | collective-permute-done | bytes 73760 | tf_op jit(solution)/shard_map/ppermute | solution.py:17
  36.3 0.7 collective-permute-done.5
  37.0 0.2 pad_maximum_fusion.11
  37.2 1.6 collective-permute-start.6
  38.8 1.4 collective-permute-start.7
  40.2 4.6 %convolution_multiply_fusion.2 = f32[18,512]{1,0:T(8,128)S(1)} fusion(bf16[8192,512]{1,0:T(8,128)(2,1)} %bitcast.24, f32[8192,18]{0,1:T(8,128)S(1)} %get-tuple-element.28), kind=kOutput, calls=%fused_computation.55 | convolution fusion | flops 151446528 | bytes 9015296 | tf_op jit(solution)/shard_map/dot_general | solution.py:70
  44.7 0.0 collective-permute-done.6
  44.8 0.0 collective-permute-done.7
  44.8 0.4 maximum_maximum_fusion
  45.2 0.7 fusion.21
  45.9 0.0 copy-start.1
  45.9 0.4 reshape.35
  46.3 0.3 copy-done.1
  46.7 5.8 %fusion.39 = (f32[18]{0:T(128)S(1)}, bf16[8192,18]{0,1:T(8,128)(2,1)S(1)}, bf16[8192,18]{0,1:T(8,128)(2,1)S(1)}, f32[8192,18]{0,1:T(8,128)S(1)}) fusion(f32[8192,18]{0,1:T(8,128)S(1)} %get-tuple-element.28, f32[8192,18]{0,1:T(8,128)S(1)} %reshape.35, bf16[8192,512]{1,0:T(8,128)(2,1)} %bitcast.25, bf16[18,512]{1,0:T(8,128)(2,1)S(1)} %copy-done.1), kind=kOutput, calls=%fused_computation.87 | convolution fusion | flops 152616944 | bytes 10766408 | tf_op jit(solution)/shard_map/dot_general | solution.py:57
  52.5 0.3 convert_reduce_fusion
  52.7 5.3 %fusion.25 = f32[512,36]{0,1:T(8,128)} fusion(bf16[8192,512]{1,0:T(8,128)(2,1)} %bitcast.27, bf16[8192,18]{0,1:T(8,128)(2,1)S(1)} %get-tuple-element.22, bf16[8192,18]{0,1:T(8,128)(2,1)S(1)} %get-tuple-element.21), kind=kOutput, calls=%fused_computation.54 | convolution fusion | flops 303187968 | bytes 9052160 | tf_op jit(solution)/shard_map/dot_general | solution.py:63
  58.0 14.6 %psum.35 = f32[18]{0:T(128)S(1)} all-reduce(f32[18]{0:T(128)S(1)} %broadcast_multiply_fusion.3), channel_id=1, replica_groups=mesh['ha'=8,'wa'=4] {'ha'}, use_global_device_ids=true, to_apply=%region_1.0 | all-reduce | flops 18 | bytes 144 | tf_op jit(solution)/shard_map/psum | solution.py:51
  72.7 0.0 all-reduce.3.cloned.1.call-update
  72.7 8.1 %psum.36 = f32[18]{0:T(128)S(1)} all-reduce(f32[18]{0:T(128)S(1)} %psum.35), channel_id=1, replica_groups=mesh['ha'=8,'wa'=4] {'wa'}, use_global_device_ids=true, to_apply=%region_2.0 | all-reduce | flops 18 | bytes 144 | tf_op jit(solution)/shard_map/psum | solution.py:51
  80.8 0.0 copy-start.2
  80.8 42.9 %all-reduce = (f32[36]{0:T(128)S(1)}, f32[18,512]{1,0:T(8,128)}) all-reduce(f32[36]{0:T(128)S(1)} %broadcast_multiply_fusion, f32[18,512]{1,0:T(8,128)S(1)} %convolution_multiply_fusion.2), channel_id=1, replica_groups=mesh['ha'=8,'wa'=4] {'ha','wa'}, use_global_device_ids=true, to_apply=%region_6.0 | all-reduce | flops 9252 | bytes 74016 | tf_op jit(solution)/shard_map/psum | solution.py:73
  123.7 0.6 multiply_subtract_fusion
  124.3 5.9 %convolution_convert_fusion = bf16[8192,512]{1,0:T(8,128)(2,1)} fusion(bf16[512,18]{0,1:T(8,128)(2,1)S(1)} %copy-done, f32[8192,18]{0,1:T(8,128)S(1)} %get-tuple-element.29, f32[8192,18]{0,1:T(8,128)S(1)} %reshape.35, f32[8192,18]{0,1:T(8,128)S(1)} %get-tuple-element.28, f32[18]{0:T(128)S(1)} %get-tuple-element.26), kind=kOutput, calls=%fused_computation | convolution fusion | flops 156221440 | bytes 10176584 | tf_op jit(solution)/shard_map/dot_general | solution.py:78
  130.2 0.0 copy-done.2
  130.2 67.1 %all-reduce.3.cloned.1.call-done = f32[512,36]{0,1:T(8,128)} async-done(((f32[512,36]{0,1:T(8,128)}), f32[512,36]{0,1:T(8,128)}) %all-reduce.3.cloned.1.call-update) | async-done | bytes 73744 | tf_op jit(solution)/shard_map/psum | solution.py:73
  197.2 1.6 fusion.32
  (7 shorter events, 0.1 us)
Async XLA Ops:
  7.2 0.7 copy-start
  7.2 190.1 %all-reduce.3.cloned.1.call-start = ((), (), s32[]{:S(2)}) async-start(), calls=%async_computation | async-start | bytes 163840 | tf_op jit(solution)/shard_map/psum | solution.py:73
  13.7 4.6 %collective-permute-start = (f32[1,16,64,18]{2,1,0,3:T(8,128)S(1)}, f32[1,16,64,18]{2,1,0,3:T(8,128)S(1)}, u32[]{:S(2)}, u32[]{:S(2)}) collective-permute-start(f32[1,16,64,18]{2,1,0,3:T(8,128)S(1)} %bitcast.29), channel_id=1, source_target_pairs={{0,4},{4,8},{8,12},{12,16},{16,20},{20,24},{24,28},{28,0},{1,5},{5... | collective-permute-start | bytes 221192 | tf_op jit(solution)/shard_map/ppermute | solution.py:17
  13.9 5.3 %collective-permute-start.1 = (f32[1,16,64,18]{2,1,0,3:T(8,128)S(1)}, f32[1,16,64,18]{2,1,0,3:T(8,128)S(1)}, u32[]{:S(2)}, u32[]{:S(2)}) collective-permute-start(f32[1,16,64,18]{2,1,0,3:T(8,128)S(1)} %bitcast.30), channel_id=1, source_target_pairs={{4,0},{8,4},{12,8},{16,12},{20,16},{24,20},{28,24},{0,28},{5,1},{9... | collective-permute-start | bytes 221192 | tf_op jit(solution)/shard_map/ppermute | solution.py:19
  19.3 6.4 %collective-permute-start.2 = (f32[10,1,64,18]{2,1,0,3:T(1,128)S(1)}, f32[10,1,64,18]{2,1,0,3:T(1,128)S(1)}, u32[]{:S(2)}, u32[]{:S(2)}) collective-permute-start(f32[10,1,64,18]{2,1,0,3:T(1,128)S(1)} %get-tuple-element.16), channel_id=1, source_target_pairs={{0,1},{1,2},{2,3},{3,0},{4,5},{5,6},{6,7},{7,4},{8,9},{9,10},{10,1... | collective-permute-start | bytes 138248 | tf_op jit(solution)/shard_map/ppermute | solution.py:17
  21.4 6.8 %collective-permute-start.3 = (f32[10,1,64,18]{2,1,0,3:T(1,128)S(1)}, f32[10,1,64,18]{2,1,0,3:T(1,128)S(1)}, u32[]{:S(2)}, u32[]{:S(2)}) collective-permute-start(f32[10,1,64,18]{2,1,0,3:T(1,128)S(1)} %get-tuple-element.17), channel_id=1, source_target_pairs={{1,0},{2,1},{3,2},{0,3},{5,4},{6,5},{7,6},{4,7},{9,8},{10,9},{11,1... | collective-permute-start | bytes 138248 | tf_op jit(solution)/shard_map/ppermute | solution.py:19
  31.7 4.6 %collective-permute-start.4 = (f32[1,16,64,18]{2,1,0,3:T(8,128)S(1)}, f32[1,16,64,18]{2,1,0,3:T(8,128)S(1)}, u32[]{:S(2)}, u32[]{:S(2)}) collective-permute-start(f32[1,16,64,18]{2,1,0,3:T(8,128)S(1)} %get-tuple-element.18), channel_id=1, source_target_pairs={{0,4},{4,8},{8,12},{12,16},{16,20},{20,24},{24,28},{28,0},{1,5},{5... | collective-permute-start | bytes 221192 | tf_op jit(solution)/shard_map/ppermute | solution.py:17
  31.8 5.3 %collective-permute-start.5 = (f32[1,16,64,18]{2,1,0,3:T(8,128)S(1)}, f32[1,16,64,18]{2,1,0,3:T(8,128)S(1)}, u32[]{:S(2)}, u32[]{:S(2)}) collective-permute-start(f32[1,16,64,18]{2,1,0,3:T(8,128)S(1)} %get-tuple-element.19), channel_id=1, source_target_pairs={{4,0},{8,4},{12,8},{16,12},{20,16},{24,20},{28,24},{0,28},{5,1},{9... | collective-permute-start | bytes 221192 | tf_op jit(solution)/shard_map/ppermute | solution.py:19
  37.2 7.6 %collective-permute-start.6 = (f32[10,1,64,18]{2,1,0,3:T(1,128)S(1)}, f32[10,1,64,18]{2,1,0,3:T(1,128)S(1)}, u32[]{:S(2)}, u32[]{:S(2)}) collective-permute-start(f32[10,1,64,18]{2,1,0,3:T(1,128)S(1)} %get-tuple-element.14), channel_id=1, source_target_pairs={{0,1},{1,2},{2,3},{3,0},{4,5},{5,6},{6,7},{7,4},{8,9},{9,10},{10,1... | collective-permute-start | bytes 138248 | tf_op jit(solution)/shard_map/ppermute | solution.py:17
  38.8 6.0 %collective-permute-start.7 = (f32[10,1,64,18]{2,1,0,3:T(1,128)S(1)}, f32[10,1,64,18]{2,1,0,3:T(1,128)S(1)}, u32[]{:S(2)}, u32[]{:S(2)}) collective-permute-start(f32[10,1,64,18]{2,1,0,3:T(1,128)S(1)} %get-tuple-element.15), channel_id=1, source_target_pairs={{1,0},{2,1},{3,2},{0,3},{5,4},{6,5},{7,6},{4,7},{9,8},{10,9},{11,1... | collective-permute-start | bytes 138248 | tf_op jit(solution)/shard_map/ppermute | solution.py:19
  45.9 0.7 copy-start.1
  80.8 49.4 %copy-start.2 = (f32[18]{0:T(128)}, f32[18]{0:T(128)S(1)}, u32[]{:S(2)}) copy-start(f32[18]{0:T(128)S(1)} %psum.36) | copy-start | bytes 220
Sparse Core Ops, SparseCore 0:
  72.8 124.3 all-reduce.2
